TPU v7x, 32 devices: a whole 2x2x4 slice. The times are simulated.
32 devices in a mesh: batch: 2 (over y), freq: 8 (over z, x), elem: 2 (over core).
Axes of the slice: x: 2, y: 2, z: 4, core: 2. Of those that a mesh axis runs over, the one named last changes fastest.
Arguments:
- flaw_cells: int32 [512], P('batch'), parts along dimension 0, may hold values from 0 to 255, each once
- flaw_blocks: int32 [16], P('batch'), parts along dimension 0, may hold values from 0 to 7, each once
- element_channel: int32 [256], P('elem'), may hold values from 0 to 255, each once
- focal_delay: float32 [256, 256], replicated, may hold values from 0 to 64
- beam_field: bfloat16 [128, 2, 256, 256], P('freq', None, 'elem'), may hold values from -0.125 to 0.125
- flaw_size: float32 [4, 128], P('batch'), parts along dimension 0, may hold values from 0.5 to 4
- flaw_slope: float32 [4, 128], P('batch'), parts along dimension 0, may hold values from 0.2 to 1
- noise_level: float32 [4, 128], P(('batch', 'elem'), 'freq'), parts along dimension 0, may hold values from 0.5 to 5
Outputs:
- flaw_peak: float32 [4, 128], P(('batch', 'elem'), 'freq'), parts along dimension 0
- detection: float32 [4, 128], P(('batch', 'elem'), 'freq'), parts along dimension 0
There are 2 independent parts, one for each index of `batch`. A program takes and returns all parts, laid end to end along the dimension named above; an argument that names none is the same for every part. Nothing has to cross between parts.
Inputs may be any that keep to these rules, and one draw needn't show every extreme that they name: `flaw_cells`: every site holds exactly one flaw. `flaw_blocks`: every scan block belongs to exactly one flaw group. `element_channel`: every channel drives exactly one element.
All inputs are finite; a program needn't handle non-finite values.
Results may differ from a plain program's by a relative error of at most 0.0011.
Values may be sent and summed in bfloat16 or wider, within the bound.
A program may use at most 64 MiB of HBM per device.

v0:
```python
import math
import jax
import jax.numpy as jnp
from jax import lax
from jax.sharding import PartitionSpec as P

W_DEV = 16
FG = 128
NB = 4
SB = 32
T_CAP = 1024
EDGE = 0.6
STEEP = 3.0
EPS = 1e-05


def kirchhoff(angular, flaw_size, flaw_slope):
    angles = angular[None, :, None] * (2.0 * flaw_size * flaw_slope)[:, None, :]
    real_part = flaw_size[:, None, :] * (1.0 + EDGE) * jnp.cos(angles)
    imag_part = flaw_size[:, None, :] * (EDGE - 1.0) * jnp.sin(angles)
    return (real_part, imag_part)


def focal_law(angular, delays):
    phases = angular[:, None, None, None] * delays[None]
    return jnp.concatenate([jnp.cos(phases), -jnp.sin(phases)], axis=-1).astype(jnp.bfloat16)


def field_matrix(fields):
    real_part = fields[:, 0]
    imag_part = fields[:, 1]
    upper_rows = jnp.concatenate([real_part, imag_part], axis=-1)
    lower_rows = jnp.concatenate([-imag_part, real_part], axis=-1)
    return jnp.concatenate([upper_rows, lower_rows], axis=1)


def combine(product, k_real, k_imag):
    columns = k_real.shape[-1]
    real_part = product[..., :columns]
    imag_part = product[..., columns:]
    scale_real = k_real[:, :, None, :]
    scale_imag = k_imag[:, :, None, :]
    return jnp.stack(
        [
            scale_real * real_part - scale_imag * imag_part,
            scale_real * imag_part + scale_imag * real_part,
        ],
        axis=2,
    )


def envelope_peak(spectra, row_count):
    groups, freq_total, planes, columns = spectra.shape
    sample_count = min(T_CAP, 2 * freq_total)
    time_block = min(128, sample_count)
    freq_index = jnp.arange(freq_total, dtype=jnp.int32)
    scaling = 1.0 / math.sqrt(freq_total)

    def advance(step_index, running):
        sample_times = step_index * time_block + jnp.arange(time_block, dtype=jnp.int32)
        phase_steps = freq_index[:, None] * sample_times[None, :] % (2 * freq_total)
        angles = phase_steps.astype(jnp.float32) * (math.pi / freq_total)
        cosine = jnp.cos(angles)
        sine_part = jnp.sin(angles)
        twiddle = jnp.stack(
            [jnp.stack([cosine, sine_part], axis=1), jnp.stack([-sine_part, cosine], axis=1)],
            axis=1,
        )
        twiddle_high = lax.optimization_barrier(twiddle.astype(jnp.bfloat16))
        twiddle_low = (twiddle - twiddle_high.astype(jnp.float32)).astype(jnp.bfloat16)
        signal = jnp.einsum(
            "gwcx,wckt->gkxt", spectra, twiddle_high, preferred_element_type=jnp.float32
        )
        signal = signal + jnp.einsum(
            "gwcx,wckt->gkxt", spectra, twiddle_low, preferred_element_type=jnp.float32
        )
        signal = signal * scaling
        magnitude = jnp.sqrt(signal[:, 0] * signal[:, 0] + signal[:, 1] * signal[:, 1])
        magnitude = magnitude.reshape(groups, row_count, columns // row_count, time_block)
        return jnp.maximum(running, jnp.max(magnitude, axis=(1, 3)))

    initial = jnp.zeros((groups, columns // row_count), jnp.float32)
    return lax.fori_loop(0, sample_count // time_block, advance, initial)


def regroup_peaks(moved):
    groups, freq_total, planes, row_count, flaw_count = moved.shape
    return envelope_peak(
        moved.reshape(groups, freq_total, planes, row_count * flaw_count), row_count
    )


def body(
    flaw_cells,
    flaw_blocks,
    element_channel,
    focal_delay,
    beam_field,
    flaw_size,
    flaw_slope,
    noise_level,
):
    freq_count = lax.axis_size("freq")
    freq_total = W_DEV * freq_count
    group_total = flaw_size.shape[0]
    row_total = NB * SB
    first_freq = lax.axis_index("freq") * W_DEV
    angular = (first_freq + jnp.arange(W_DEV, dtype=jnp.int32)).astype(jnp.float32) * (
        math.pi / freq_total
    )
    scan_rows = (
        flaw_blocks.reshape(group_total, NB)[:, :, None] * SB
        + jnp.arange(SB, dtype=jnp.int32)[None, None, :]
    ).reshape(group_total, row_total)
    delays = jnp.moveaxis(
        jnp.take(jnp.take(focal_delay, element_channel, axis=0), scan_rows, axis=1), 0, 2
    )
    fields = jnp.take(beam_field, flaw_cells, axis=3).reshape(
        W_DEV, 2, element_channel.shape[0], group_total, FG
    )
    k_real, k_imag = kirchhoff(angular, flaw_size, flaw_slope)
    focal_terms = focal_law(angular, delays)
    field_terms = field_matrix(fields)
    product = jnp.einsum(
        "wgre,wegf->gwrf", focal_terms, field_terms, preferred_element_type=jnp.float32
    )
    partial_value = combine(product, k_real, k_imag).astype(jnp.bfloat16)
    rounded_term = lax.optimization_barrier(partial_value).astype(jnp.float32)
    summed = lax.psum_scatter(
        rounded_term.astype(jnp.bfloat16), "elem", scatter_dimension=0, tiled=True
    )
    partial_peak = regroup_peaks(
        lax.all_to_all(summed, "freq", split_axis=3, concat_axis=1, tiled=True)
    )
    whole_peak = lax.pmax(partial_peak, "freq")
    columns = FG // freq_count
    flaw_peak = lax.dynamic_slice_in_dim(whole_peak, lax.axis_index("freq") * columns, columns, 1)
    detection = jax.nn.sigmoid(STEEP * (jnp.log(flaw_peak + EPS) - jnp.log(noise_level)))
    return (flaw_peak, detection)


def solution(mesh):
    in_specs = (
        P("batch"),
        P("batch"),
        P("elem"),
        P(),
        P("freq", None, "elem", None),
        P("batch", None),
        P("batch", None),
        P(("batch", "elem"), "freq"),
    )
    out_specs = (P(("batch", "elem"), "freq"), P(("batch", "elem"), "freq"))
    return jax.shard_map(body, mesh=mesh, in_specs=in_specs, out_specs=out_specs, check_vma=False)
```

profile of v0, /device:TPU:0, one launch (start us, length us, event | category | flops | bytes accessed | tf_op | source)
XLA Modules:
  0.0 130.7 jit_solution(10028995258592045228)
XLA Ops:
  7.2 0.7 compare_select_fusion.3
  7.9 1.2 compare_and_fusion
  9.1 0.7 broadcast_multiply_fusion.2
  10.1 0.7 compare_select_fusion
  10.8 0.7 and_bitcast_fusion
  11.4 3.5 %copy.28 = bf16[16,2,128,256]{2,0,3,1:T(8,128)(2,1)S(1)} copy(bf16[16,2,128,256]{3,2,1,0:T(8,128)(2,1)} %param.14) | data formatting | bytes 4194304 | tf_op args[4]
  14.9 2.3 %gather_fusion.2 = bf16[256,16,2,128]{3,1,2,0:T(8,128)(2,1)} fusion(bf16[16,2,128,256]{2,0,3,1:T(8,128)(2,1)S(1)} %copy.28, s32[1024]{0:T(1024)S(1)} %pad_clamp_fusion), kind=kCustom, calls=%fused_computation.2 | custom fusion | bytes 4195328 | tf_op jit(solution)/shard_map/jit(_take)/gather | solution.py:118
  17.2 3.5 %copy.30 = bf16[16,2,128,2,128]{4,2,0,3,1:T(8,128)(2,1)S(1)} copy(bf16[16,2,128,2,128]{2,0,1,4,3:T(8,128)(2,1)} %bitcast.85) | data formatting | bytes 4194304 | tf_op jit(solution)/shard_map/jit(_take)/gather | solution.py:118
  21.3 0.8 gather_fusion
  22.1 1.4 %broadcast_select_fusion.3 = f32[128,256]{1,0:T(8,128)} fusion(f32[128,256]{1,0:T(8,128)S(1)} %gather_fusion, pred[128]{0:T(512)(128)(4,1)} %compare_and_fusion), kind=kLoop, calls=%fused_computation.64 | loop fusion | flops 32768 | bytes 262272 | tf_op jit(solution)/shard_map/jit(_take)/select_n | solution.py:116
  23.5 1.0 copy.27
  24.5 0.5 compare_and_fusion.1
  25.0 1.3 %gather_fusion.1 = f32[256,128]{1,0:T(8,128)} fusion(f32[128,256]{0,1:T(8,128)S(1)} %copy.27, s32[1024]{0:T(1024)S(1)} %pad_clamp_fusion.1), kind=kCustom, calls=%fused_computation.1 | custom fusion | bytes 263168 | tf_op jit(solution)/shard_map/jit(_take)/gather | solution.py:116
  26.3 1.0 broadcast_select_fusion.2
  27.3 7.8 %fusion.30 = (bf16[16,2,128,128]{3,2,0,1:T(8,128)(2,1)S(1)}, bf16[16,2,128,128]{3,2,0,1:T(8,128)(2,1)S(1)}) fusion(f32[2,128,128]{2,1,0:T(8,128)S(1)} %broadcast_select_fusion.2, f32[16]{0:T(128)S(1)} %convert_multiply_fusion), kind=kLoop, calls=%fused_computation.49 | loop fusion | flops 2097152 | bytes 2228288 | tf_op jit(solution)/shard_map/convert.4
  35.1 0.7 broadcast_multiply_fusion.1
  36.0 1.4 %fusion.22 = f32[2,16,128,256]{3,2,1,0:T(8,128)S(1)} fusion(bf16[16,128,2,128]{3,1,0,2:T(8,128)(2,1)S(1)} %get-tuple-element.144, bf16[16,128,2,128]{3,1,0,2:T(8,128)(2,1)S(1)} %fusion.42, bf16[16,128,2,128]{3,1,0,2:T(8,128)(2,1)S(1)} %get-tuple-element.143, bf16[16,2,128,128]{3,2,0,1:T(8,128)(2,1)S(1)} %get-tuple-element.146, ...), kind=kOutput, calls=%fused_computation.39 | convolution fusion | flops 557842432 | bytes 9437184 | tf_op jit(solution)/shard_map/wgre,wegf->gwrf/dot_general | solution.py:124
  37.4 0.6 fusion.36
  38.1 1.5 %pad_maximum_fusion.1 = bf16[2,16,2,128,128]{4,3,1,0,2:T(8,128)(2,1)} fusion(bf16[2,16,1,128,128]{4,3,1,0,2:T(8,128)(2,1)S(1)} %get-tuple-element.142, bf16[2,16,1,128,128]{4,3,1,0,2:T(8,128)(2,1)S(1)} %get-tuple-element.141), kind=kLoop, calls=%fused_computation.55 | loop fusion | flops 1048576 | bytes 4194304 | tf_op jit(solution)/shard_map/stack | solution.py:43
  39.6 0.6 copy-done.2
  40.2 0.6 dynamic-slice
  40.8 22.9 %all-reduce.3.cloned.1.call-done = bf16[2,16,2,128,128]{4,3,1,0,2:T(8,128)(2,1)} async-done(((bf16[2,16,2,128,128]{4,3,1,0,2:T(8,128)(2,1)}), bf16[2,16,2,128,128]{4,3,1,0,2:T(8,128)(2,1)}) %all-reduce.3.cloned.1.call-update) | async-done | bytes 2097168
  63.6 1.9 %constant_dynamic-slice_fusion = bf16[1,16,2,128,128]{4,3,1,0,2:T(8,128)(2,1)S(1)} fusion(bf16[2,16,2,128,128]{4,3,1,0,2:T(8,128)(2,1)} %all-reduce.3.cloned.1.call-done, u32[]{:T(128)} %bitcast.34), kind=kLoop, calls=%fused_computation.81 | loop fusion | bytes 2097156
  65.6 1.7 %copy.31 = bf16[1,16,2,128,128]{4,1,0,2,3:T(8,128)(2,1)} copy(bf16[1,16,2,128,128]{4,3,1,0,2:T(8,128)(2,1)S(1)} %constant_dynamic-slice_fusion) | data formatting | bytes 2097152 | tf_op jit(solution)/shard_map/reduce_scatter | solution.py:129
  67.2 5.8 %all-to-all-start = ((bf16[1,16,2,128,128]{4,1,0,2,3:T(8,128)(2,1)}), bf16[1,16,2,128,128]{4,1,0,2,3:T(8,128)(2,1)S(1)}, u32[]{:S(2)}, u32[]{:S(2)}) async-start(bf16[1,16,2,128,128]{4,1,0,2,3:T(8,128)(2,1)} %copy.31), calls=%async_computation | async-start | bytes 2097152 | tf_op jit(solution)/shard_map/all_to_all | solution.py:133
  73.0 26.2 %all-to-all-done = bf16[1,16,2,128,128]{4,1,0,2,3:T(8,128)(2,1)S(1)} async-done(((bf16[1,16,2,128,128]{4,1,0,2,3:T(8,128)(2,1)}), bf16[1,16,2,128,128]{4,1,0,2,3:T(8,128)(2,1)S(1)}, u32[]{:S(2)}, u32[]{:S(2)}) %all-to-all-start) | async-done | bytes 1048608 | tf_op jit(solution)/shard_map/all_to_all | solution.py:133
  99.7 0.5 reshape.333
  100.2 3.5 %while.16 = (s32[]{:T(128)}, f32[1,128]{1,0:T(1,128)S(1)}, bf16[1,128,2,2048]{3,1,2,0:T(8,128)(2,1)S(1)}, s32[]{:T(128)}, s32[]{:T(128)}, /*index=5*/s32[]{:T(128)}) while((s32[]{:T(128)}, f32[1,128]{1,0:T(1,128)S(1)}, bf16[1,128,2,2048]{3,1,2,0:T(8,128)(2,1)S(1)}, s32[]{:T(128)}, s32[]{:T(128)}, /*index=5*/s32[]{:T(128)}) %tuple.58), condition=%wide.region_4.5_spmd.clone, body=%wide.region_1.4_spmd.clone.sunk | while | flops 539607296 | bytes 12078175 | solution.py:83
  101.0 0.5 fusion.57
  102.8 0.5 fusion.57
  103.7 19.5 %pmax.7 = f32[1,128]{1,0:T(1,128)S(1)} all-reduce(f32[1,128]{1,0:T(1,128)S(1)} %get-tuple-element.113), channel_id=1, replica_groups=mesh['batch'=2,'freq'=8,'elem'=2] {'freq'}, use_global_device_ids=true, to_apply=%region_5.6 | all-reduce | flops 128 | bytes 1024 | tf_op jit(solution)/shard_map/pmax | solution.py:135
  123.2 0.6 add_divide_fusion
  (40 shorter events, 4.0 us)
Async XLA Ops:
  7.2 14.1 %copy-start = (f32[256,256]{1,0:T(8,128)S(1)}, f32[256,256]{1,0:T(8,128)}, u32[]{:S(2)}) copy-start(f32[256,256]{1,0:T(8,128)} %param.13) | copy-start | bytes 786436
  7.2 56.5 %all-reduce.3.cloned.1.call-start = ((), (), s32[]{:S(2)}) async-start(), calls=%async_computation.1 | async-start | bytes 4194304
  39.5 0.7 copy-start.2
  67.2 32.0 %all-to-all-start = ((bf16[1,16,2,128,128]{4,1,0,2,3:T(8,128)(2,1)}), bf16[1,16,2,128,128]{4,1,0,2,3:T(8,128)(2,1)S(1)}, u32[]{:S(2)}, u32[]{:S(2)}) async-start(bf16[1,16,2,128,128]{4,1,0,2,3:T(8,128)(2,1)} %copy.31), calls=%async_computation | async-start | bytes 2097152 | tf_op jit(solution)/shard_map/all_to_all | solution.py:133
  100.2 23.0 %copy-start.1 = (f32[1,16]{1,0:T(1,128)S(1)}, f32[1,16]{1,0:T(1,128)}, u32[]{:S(2)}) copy-start(f32[1,16]{1,0:T(1,128)} %param.17) | copy-start | bytes 196
Sparse Core Ops, SparseCore 0:
  39.7 23.9 all-reduce.2
where the time goes:
time: 131 us
  waiting for transfers between devices  49.1 us (37%)
  other arithmetic  20.2 us (15%)
  blocking collectives  19.5 us (15%)
  local copies, waits for them, and re-layouts  18.6 us (14%)
  between operations  14.2 us (11%)
  starting transfers between devices  5.81 us (4%)
  matrix products  3.2 us (2%)
    all_to_all x1, waiting for transfers between devices, body(): lax.all_to_all(summed, 'freq', split_axis=3, concat_axis=1, tiled=True)  26.2 us
    unnamed x2, waiting for transfers between devices  22.9 us
    pmax x1, blocking collectives, body(): whole_peak = lax.pmax(partial_peak, 'freq')  19.5 us
    another operation x1, other arithmetic  7.81 us
    unnamed x9, local copies, waits for them, and re-layouts  6.63 us
    all_to_all x1, starting transfers between devices, body(): lax.all_to_all(summed, 'freq', split_axis=3, concat_axis=1, tiled=True)  5.78 us
    gather x2, local copies, waits for them, and re-layouts, body(): jnp.take(beam_field, flaw_cells, axis=3)  5.75 us
  transfers between devices with their start and end apart: 2, of which 2 were waited for; matrix products, arithmetic and copies ran while one was open for 0% of the time, Pallas kernels for 0%

commit v1 on v0

--- a/solution.py
+++ b/solution.py
@@ -3,6 +3,7 @@
 import jax.numpy as jnp
 from jax import lax
 from jax.sharding import PartitionSpec as P
+from jax.lax import all_to_all, axis_size
 
 W_DEV = 16
 FG = 128
@@ -129,9 +130,11 @@
     summed = lax.psum_scatter(
         rounded_term.astype(jnp.bfloat16), "elem", scatter_dimension=0, tiled=True
     )
-    partial_peak = regroup_peaks(
-        lax.all_to_all(summed, "freq", split_axis=3, concat_axis=1, tiled=True)
+    map_widths = lambda unit, shard_axis: jnp.concatenate(
+        all_to_all(jnp.stack(jnp.split(unit, axis_size(shard_axis), axis=3)), shard_axis, 0, 0),
+        axis=1,
     )
+    partial_peak = regroup_peaks(map_widths(summed, shard_axis="freq"))
     whole_peak = lax.pmax(partial_peak, "freq")
     columns = FG // freq_count
     flaw_peak = lax.dynamic_slice_in_dim(whole_peak, lax.axis_index("freq") * columns, columns, 1)

time: 131 us -> 136 us (1.038)
  local copies, waits for them, and re-layouts: 18.6 us -> 23.7 us
    another operation x0 -> x2, local copies, waits for them, and re-layouts: none -> 2.76 us  [the longest x1 2.27 us: body(): jnp.stack(jnp.split(unit, axis_size(shard_axis), axis=3))]
    unnamed x9 -> x15, local copies, waits for them, and re-layouts: 6.63 us -> 9.36 us
where the time goes in v1:
time: 136 us
  waiting for transfers between devices  49.1 us (36%)
  local copies, waits for them, and re-layouts  23.7 us (17%)
  other arithmetic  20.2 us (15%)
  blocking collectives  19.5 us (14%)
  between operations  14.2 us (10%)
  starting transfers between devices  5.81 us (4%)
  matrix products  3.2 us (2%)
    all_to_all x1, waiting for transfers between devices, body(): all_to_all(jnp.stack(jnp.split(unit, axis_size(shard_axis), axis=3)), sha...  26.2 us
    unnamed x2, waiting for transfers between devices  22.9 us
    pmax x1, blocking collectives, body(): whole_peak = lax.pmax(partial_peak, 'freq')  19.5 us
    unnamed x15, local copies, waits for them, and re-layouts  9.36 us
    another operation x1, other arithmetic  7.81 us
    all_to_all x1, starting transfers between devices, body(): all_to_all(jnp.stack(jnp.split(unit, axis_size(shard_axis), axis=3)), sha...  5.78 us
    gather x2, local copies, waits for them, and re-layouts, body(): jnp.take(beam_field, flaw_cells, axis=3)  5.76 us
  transfers between devices with their start and end apart: 2, of which 2 were waited for; matrix products, arithmetic and copies ran while one was open for 0% of the time, Pallas kernels for 0%

profile of v1, /device:TPU:0, one launch (start us, length us, event | category | flops | bytes accessed | tf_op | source)
XLA Modules:
  0.0 135.8 jit_solution(12490831925255874524)
XLA Ops:
  7.2 0.7 compare_select_fusion.3
  7.9 1.2 compare_and_fusion
  9.1 0.7 broadcast_multiply_fusion.2
  10.1 0.7 compare_select_fusion
  10.8 0.7 and_bitcast_fusion
  11.5 3.5 %copy.47 = bf16[16,2,128,256]{2,0,3,1:T(8,128)(2,1)S(1)} copy(bf16[16,2,128,256]{3,2,1,0:T(8,128)(2,1)} %param.14) | data formatting | bytes 4194304 | tf_op args[4]
  15.0 2.3 %gather_fusion.2 = bf16[256,16,2,128]{3,1,2,0:T(8,128)(2,1)} fusion(bf16[16,2,128,256]{2,0,3,1:T(8,128)(2,1)S(1)} %copy.47, s32[1024]{0:T(1024)S(1)} %get-tuple-element.152), kind=kCustom, calls=%fused_computation.2 | custom fusion | bytes 4195328 | tf_op jit(solution)/shard_map/jit(_take)/gather | solution.py:119
  17.3 3.5 %copy.49 = bf16[16,2,128,2,128]{4,2,0,3,1:T(8,128)(2,1)S(1)} copy(bf16[16,2,128,2,128]{2,0,1,4,3:T(8,128)(2,1)} %bitcast.122) | data formatting | bytes 4194304 | tf_op jit(solution)/shard_map/jit(_take)/gather | solution.py:119
  21.3 0.8 gather_fusion
  22.1 1.4 %broadcast_select_fusion.3 = f32[128,256]{1,0:T(8,128)} fusion(f32[128,256]{1,0:T(8,128)S(1)} %gather_fusion, pred[128]{0:T(512)(128)(4,1)} %compare_and_fusion), kind=kLoop, calls=%fused_computation.81 | loop fusion | flops 32768 | bytes 262272 | tf_op jit(solution)/shard_map/jit(_take)/select_n | solution.py:117
  23.5 1.0 copy.46
  25.0 1.3 gather_fusion.1
  26.3 1.0 broadcast_select_fusion.2
  27.4 7.8 %fusion.30 = (bf16[16,2,128,128]{3,2,0,1:T(8,128)(2,1)S(1)}, bf16[16,2,128,128]{3,2,0,1:T(8,128)(2,1)S(1)}) fusion(f32[2,128,128]{2,1,0:T(8,128)S(1)} %broadcast_select_fusion.2, f32[16]{0:T(128)S(1)} %convert_multiply_fusion), kind=kLoop, calls=%fused_computation.49 | loop fusion | flops 2097152 | bytes 2228288 | tf_op jit(solution)/shard_map/convert.4
  35.2 0.7 broadcast_multiply_fusion.1
  36.0 1.4 %fusion.22 = f32[2,16,128,256]{3,2,1,0:T(8,128)S(1)} fusion(bf16[16,128,2,128]{3,1,0,2:T(8,128)(2,1)S(1)} %get-tuple-element.144, bf16[16,128,2,128]{3,1,0,2:T(8,128)(2,1)S(1)} %fusion.50, bf16[16,128,2,128]{3,1,0,2:T(8,128)(2,1)S(1)} %get-tuple-element.143, bf16[16,2,128,128]{3,2,0,1:T(8,128)(2,1)S(1)} %get-tuple-element.146, ...), kind=kOutput, calls=%fused_computation.39 | convolution fusion | flops 557842432 | bytes 9437184 | tf_op jit(solution)/shard_map/wgre,wegf->gwrf/dot_general | solution.py:125
  37.4 0.6 fusion.36
  38.1 1.5 %pad_maximum_fusion.1 = bf16[2,16,2,128,128]{4,3,1,0,2:T(8,128)(2,1)} fusion(bf16[2,16,1,128,128]{4,3,1,0,2:T(8,128)(2,1)S(1)} %get-tuple-element.142, bf16[2,16,1,128,128]{4,3,1,0,2:T(8,128)(2,1)S(1)} %get-tuple-element.141), kind=kLoop, calls=%fused_computation.55 | loop fusion | flops 1048576 | bytes 4194304 | tf_op jit(solution)/shard_map/stack | solution.py:44
  40.8 22.9 %all-reduce.3.cloned.1.call-done = bf16[2,16,2,128,128]{4,3,1,0,2:T(8,128)(2,1)} async-done(((bf16[2,16,2,128,128]{4,3,1,0,2:T(8,128)(2,1)}), bf16[2,16,2,128,128]{4,3,1,0,2:T(8,128)(2,1)}) %all-reduce.3.cloned.1.call-update) | async-done | bytes 2097168
  63.7 1.9 %dynamic-slice_bitcast_fusion = bf16[1,16,2,128,128]{4,3,1,2,0:T(8,128)(2,1)S(1)} fusion(bf16[2,16,2,128,128]{4,3,1,0,2:T(8,128)(2,1)} %all-reduce.3.cloned.1.call-done, u32[]{:T(128)} %bitcast.47), kind=kLoop, calls=%fused_computation.63 | loop fusion | bytes 2097156 | tf_op jit(solution)/shard_map/reduce_scatter | solution.py:130
  65.6 0.7 fusion.45
  66.3 0.7 fusion.44
  67.0 0.7 fusion.43
  67.6 0.7 fusion.42
  68.3 0.7 fusion.41
  69.0 0.7 fusion.40
  69.6 0.7 fusion.39
  70.3 2.3 %fusion.38 = bf16[8,1,16,2,16,128]{5,4,2,3,1,0:T(8,128)(2,1)} fusion(bf16[8,1,16,2,16,128]{5,4,2,3,1,0:T(8,128)(2,1)} %fusion.39, bf16[2,16,2,128,128]{4,3,1,0,2:T(8,128)(2,1)} %all-reduce.3.cloned.1.call-done, u32[]{:T(128)} %bitcast.47, u32[]{:T(128)S(6)} %convert.21), kind=kLoop, calls=%fused_computation.65 | loop fusion | bytes 262660 | tf_op jit(solution)/shard_map/stack | solution.py:134
  72.6 5.8 %all-to-all-start = ((bf16[8,1,16,2,16,128]{5,4,2,3,1,0:T(8,128)(2,1)}), bf16[8,1,16,2,16,128]{5,4,2,3,1,0:T(8,128)(2,1)S(1)}, u32[]{:S(2)}, u32[]{:S(2)}) async-start(bf16[8,1,16,2,16,128]{5,4,2,3,1,0:T(8,128)(2,1)} %fusion.38), calls=%async_computation | async-start | bytes 2097152 | tf_op jit(solution)/shard_map/all_to_all | solution.py:134
  78.3 26.2 %all-to-all-done = bf16[8,1,16,2,16,128]{5,4,2,3,1,0:T(8,128)(2,1)S(1)} async-done(((bf16[8,1,16,2,16,128]{5,4,2,3,1,0:T(8,128)(2,1)}), bf16[8,1,16,2,16,128]{5,4,2,3,1,0:T(8,128)(2,1)S(1)}, u32[]{:S(2)}, u32[]{:S(2)}) %all-to-all-start) | async-done | bytes 1048608 | tf_op jit(solution)/shard_map/all_to_all | solution.py:134
  105.3 3.5 %while.16 = (s32[]{:T(128)}, f32[1,128]{1,0:T(1,128)S(1)}, bf16[1,128,2,2048]{3,1,2,0:T(8,128)(2,1)S(1)}, s32[]{:T(128)}, s32[]{:T(128)}, /*index=5*/s32[]{:T(128)}) while((s32[]{:T(128)}, f32[1,128]{1,0:T(1,128)S(1)}, bf16[1,128,2,2048]{3,1,2,0:T(8,128)(2,1)S(1)}, s32[]{:T(128)}, s32[]{:T(128)}, /*index=5*/s32[]{:T(128)}) %tuple.59), condition=%wide.region_4.5_spmd.clone, body=%wide.region_1.4_spmd.clone.sunk | while | flops 539607296 | bytes 12078175 | solution.py:84
  108.9 19.5 %pmax.7 = f32[1,128]{1,0:T(1,128)S(1)} all-reduce(f32[1,128]{1,0:T(1,128)S(1)} %get-tuple-element.113), channel_id=1, replica_groups=mesh['batch'=2,'freq'=8,'elem'=2] {'freq'}, use_global_device_ids=true, to_apply=%region_5.6 | all-reduce | flops 128 | bytes 1024 | tf_op jit(solution)/shard_map/pmax | solution.py:138
  (46 shorter events, 7.6 us)
Async XLA Ops:
  7.2 14.2 %copy-start = (f32[256,256]{1,0:T(8,128)S(1)}, f32[256,256]{1,0:T(8,128)}, u32[]{:S(2)}) copy-start(f32[256,256]{1,0:T(8,128)} %param.13) | copy-start | bytes 786436
  7.2 56.5 %all-reduce.3.cloned.1.call-start = ((), (), s32[]{:S(2)}) async-start(), calls=%async_computation.1 | async-start | bytes 4194304
  39.6 0.7 copy-start.2
  72.6 32.0 %all-to-all-start = ((bf16[8,1,16,2,16,128]{5,4,2,3,1,0:T(8,128)(2,1)}), bf16[8,1,16,2,16,128]{5,4,2,3,1,0:T(8,128)(2,1)S(1)}, u32[]{:S(2)}, u32[]{:S(2)}) async-start(bf16[8,1,16,2,16,128]{5,4,2,3,1,0:T(8,128)(2,1)} %fusion.38), calls=%async_computation | async-start | bytes 2097152 | tf_op jit(solution)/shard_map/all_to_all | solution.py:134
  105.3 23.0 %copy-start.1 = (f32[1,16]{1,0:T(1,128)S(1)}, f32[1,16]{1,0:T(1,128)}, u32[]{:S(2)}) copy-start(f32[1,16]{1,0:T(1,128)} %param.17) | copy-start | bytes 196
Sparse Core Ops, SparseCore 0:
  39.7 23.9 all-reduce.2
